TPU v7x, 256 devices: a whole 4x4x8 slice. The times are simulated.
256 devices in a mesh: ctx: 128 (over y, x, z), tp: 2 (over core).
Axes of the slice: x: 4, y: 4, z: 8, core: 2. Of those that a mesh axis runs over, the one named last changes fastest.
Arguments:
- hidden: bfloat16 [32768, 4096], P('ctx', 'tp'), may hold values from -6 to 6
- w_query: bfloat16 [4096, 4096], P('ctx', 'tp'), may hold values from -0.09375 to 0.09375
- key_weight: bfloat16 [4096, 256], P('ctx', 'tp'), may hold values from -0.09375 to 0.09375
- value_weight: bfloat16 [4096, 256], P('ctx', 'tp'), may hold values from -0.09375 to 0.09375
- q_gain: float32 [128], replicated, may hold values from 0.5 to 2
- key_norm_gain: float32 [128], replicated, may hold values from 0.5 to 2
- earlier_keys: bfloat16 [131072, 256], P('ctx', 'tp'), may hold values from -288 to 288
- earlier_values: bfloat16 [131072, 256], P('ctx', 'tp'), may hold values from -6 to 6
- counts: int32 [64], replicated, may hold values from 1 to 16, as said below
- place: int32 [64, 16], replicated, may hold values from 0 to 15, as said below
Outputs:
- attended: bfloat16 [32768, 4096], P('ctx', 'tp')
- new_keys: bfloat16 [32768, 256], P('ctx', 'tp')
- new_values: bfloat16 [32768, 256], P('ctx', 'tp')
Inputs may be any that keep to these rules, and one draw needn't show every extreme that they name: `counts`: 16 for one trajectory and 1 for another in every draw; most trajectories have few blocks. `place`: each row orders all 16 slots of the trajectory; the slots after the first counts[b] hold stale data.
All inputs are finite; a program needn't handle non-finite values.
Results may differ from a plain program's by a relative error of at most 0.007.
Values may be sent and summed in bfloat16 or wider, within the bound.
A program may use at most 64 MiB of HBM per device.

v0:
```python
import math
import jax
import jax.numpy as jnp
from jax import lax
from jax.sharding import PartitionSpec as P

HEAD_SIZE = 128
BLOCK_TOKENS = 128


def from_partner(value, axis, apart):
    mask = 2**apart
    pairs = [(source, source ^ mask) for source in range(lax.axis_size(axis))]
    return lax.ppermute(value, axis, pairs)


def normalize_and_turn(values, gain, token_position):
    width = values.shape[-1]
    half = width // 2
    scaled = values * lax.rsqrt(jnp.mean(values * values, axis=-1, keepdims=True) + 1e-06) * gain
    freq = jnp.exp(jnp.arange(half, dtype=jnp.float32) * (-2.0 / width) * math.log(1000000.0))
    angle = token_position.astype(jnp.float32)[:, None] * freq[None, :]
    cosine = jnp.cos(angle)[:, None, :]
    sine = jnp.sin(angle)[:, None, :]
    leading_index = scaled[..., :half]
    second = scaled[..., half:]
    return jnp.concatenate(
        [leading_index * cosine - second * sine, second * cosine + leading_index * sine], axis=-1
    )


def in_order(mine, theirs, lower):
    return jnp.where(
        lower, jnp.concatenate([mine, theirs], axis=0), jnp.concatenate([theirs, mine], axis=0)
    )


def on_device(
    hidden,
    w_query,
    key_weight,
    value_weight,
    q_gain,
    key_norm_gain,
    earlier_keys,
    earlier_values,
    counts,
    place,
):
    lower = lax.axis_index("ctx") % 2 == 0
    traj_id = lax.axis_index("ctx") // 2
    whole = lax.all_gather(hidden, "tp", axis=1, tiled=True)
    tok_rows = whole.shape[0]

    def add_rows(piece):
        return jnp.dot(whole, piece, preferred_element_type=jnp.float32)

    query = add_rows(lax.all_gather(w_query, "ctx", axis=0, tiled=True))
    key_projected = add_rows(lax.all_gather(key_weight, "ctx", axis=0, tiled=True))
    value_projected = add_rows(lax.all_gather(value_weight, "ctx", axis=0, tiled=True))
    heads_q = w_query.shape[1] // HEAD_SIZE
    heads_kv = key_weight.shape[1] // HEAD_SIZE
    count = lax.dynamic_index_in_dim(counts, traj_id, 0, keepdims=False)
    offsets = lax.axis_index("ctx") % 2 * tok_rows + jnp.arange(tok_rows, dtype=jnp.int32)
    token_position = count * BLOCK_TOKENS + offsets
    rotated = normalize_and_turn(
        query.reshape(tok_rows, heads_q, HEAD_SIZE), q_gain, token_position
    ).astype(jnp.bfloat16)
    keys_mine = (
        normalize_and_turn(
            key_projected.reshape(tok_rows, heads_kv, HEAD_SIZE), key_norm_gain, token_position
        )
        .astype(jnp.bfloat16)
        .reshape(tok_rows, heads_kv * HEAD_SIZE)
    )
    values_mine = value_projected.astype(jnp.bfloat16)
    other_ck, other_cv, keys_other, values_other = from_partner(
        (earlier_keys, earlier_values, keys_mine, values_mine), "ctx", 0
    )
    keys_all = jnp.concatenate(
        [in_order(earlier_keys, other_ck, lower), in_order(keys_mine, keys_other, lower)], axis=0
    )
    vals_all = jnp.concatenate(
        [in_order(earlier_values, other_cv, lower), in_order(values_mine, values_other, lower)],
        axis=0,
    )
    slot_total = place.shape[1]
    cache_rows = slot_total * BLOCK_TOKENS
    order = lax.dynamic_index_in_dim(place, traj_id, 0, keepdims=False)
    used = jnp.arange(slot_total, dtype=jnp.int32) < count
    live = jnp.any(
        (order[:, None] == jnp.arange(slot_total, dtype=jnp.int32)[None, :]) & used[:, None], axis=0
    )
    live_tok = jnp.repeat(live, BLOCK_TOKENS)
    stretch_pos = jnp.arange(2 * tok_rows, dtype=jnp.int32)
    query_group = heads_q // heads_kv
    rows_total = query_group * tok_rows
    block_rows = min(rows_total, 512)
    block_count = rows_total // block_rows
    starts = jnp.arange(block_count, dtype=jnp.int32) * block_rows
    query_rows = jnp.transpose(rotated, (1, 0, 2)).reshape(block_count, block_rows, HEAD_SIZE)

    def attend(operands):
        block, begin = operands
        token = (begin + jnp.arange(block_rows, dtype=jnp.int32)) % tok_rows
        own_pos = lax.axis_index("ctx") % 2 * tok_rows + token
        score = lax.dot_general(
            block, keys_all, (((1,), (1,)), ((), ())), preferred_element_type=jnp.float32
        ) * HEAD_SIZE ** (-0.5)
        allowed = jnp.concatenate(
            [
                jnp.broadcast_to(live_tok[None, :], (block_rows, cache_rows)),
                stretch_pos[None, :] <= own_pos[:, None],
            ],
            axis=1,
        )
        score = jnp.where(allowed, score, -jnp.inf)
        top = jnp.max(score, axis=-1, keepdims=True)
        weight = jnp.exp(score - top)
        total = jnp.sum(weight, axis=-1, keepdims=True)
        mixed = (
            jnp.dot(weight.astype(jnp.bfloat16), vals_all, preferred_element_type=jnp.float32)
            / total
        )
        return mixed.astype(jnp.bfloat16)

    result = lax.map(attend, (query_rows, starts))
    outputs = jnp.transpose(result.reshape(query_group, tok_rows, HEAD_SIZE), (1, 0, 2))
    attended = outputs.reshape(tok_rows, heads_q * HEAD_SIZE)
    return (attended, keys_mine, values_mine)


def solution(mesh):
    placed = (
        P("ctx", "tp"),
        P("ctx", "tp"),
        P("ctx", "tp"),
        P("ctx", "tp"),
        P(),
        P(),
        P("ctx", "tp"),
        P("ctx", "tp"),
        P(),
        P(),
    )
    return jax.shard_map(
        on_device,
        mesh=mesh,
        in_specs=placed,
        out_specs=(P("ctx", "tp"), P("ctx", "tp"), P("ctx", "tp")),
        check_vma=False,
    )
```

profile of v0, /device:TPU:1, one launch (start us, length us, event | category | flops | bytes accessed | tf_op | source)
XLA Modules:
  0.0 450.9 jit_solution(13506586590148056657)
XLA Ops:
  10.0 2.6 collective-permute-start
  12.6 1.2 dynamic_slice.25
  16.6 1.2 collective-permute-done
  17.8 1.2 maximum_select_fusion
  19.0 4.4 collective-permute-done.2
  23.6 90.1 %all-gather.9.cloned.1.call-done = bf16[4096,128]{1,0:T(8,128)(2,1)} async-done(((bf16[32,128]{1,0:T(8,128)(2,1)}), bf16[4096,128]{1,0:T(8,128)(2,1)}) %all-gather.9.cloned.1.call-update) | async-done | bytes 1048592 | tf_op jit(solution)/shard_map/all_gather | solution.py:59
  113.7 21.4 %all-gather.5.cloned.1.call-done = bf16[256,4096]{1,0:T(8,128)(2,1)} async-done(((bf16[256,2048]{1,0:T(8,128)(2,1)}), bf16[256,4096]{1,0:T(8,128)(2,1)}) %all-gather.5.cloned.1.call-update) | async-done | bytes 2097168 | tf_op jit(solution)/shard_map/all_gather | solution.py:52
  135.2 2.8 multiply_reduce_fusion.1
  140.7 96.9 %all-gather.11.cloned.1.call-done = bf16[4096,128]{1,0:T(8,128)(2,1)} async-done(((bf16[32,128]{1,0:T(8,128)(2,1)}), bf16[4096,128]{1,0:T(8,128)(2,1)}) %all-gather.11.cloned.1.call-update) | async-done | bytes 1048592 | tf_op jit(solution)/shard_map/all_gather | solution.py:60
  237.6 2.1 convolution_convert_fusion
  239.7 1.6 copy.49
  242.0 1.2 collective-permute-start.3
  243.2 1.6 maximum_select_fusion.2
  244.8 1.7 copy.45
  246.5 1.6 maximum_select_fusion.3
  248.1 1.7 copy.47
  249.7 1.8 pad_maximum_fusion
  252.5 141.8 %all-gather.7.cloned.1.call-done = bf16[4096,2048]{1,0:T(8,128)(2,1)} async-done(((bf16[32,2048]{1,0:T(8,128)(2,1)}), bf16[4096,2048]{1,0:T(8,128)(2,1)}) %all-gather.7.cloned.1.call-update) | async-done | bytes 16777232 | tf_op jit(solution)/shard_map/all_gather | solution.py:58
  394.3 8.2 %convolution_bitcast_fusion = f32[32,8,16,128]{3,1,2,0:T(8,128)S(1)} fusion(bf16[256,4096]{1,0:T(8,128)(2,1)S(1)} %copy-done.1, bf16[4096,2048]{1,0:T(8,128)(2,1)} %all-gather.7.cloned.1.call-done), kind=kOutput, calls=%fused_computation.26 | convolution fusion | flops 4294967296 | bytes 20971520 | tf_op jit(solution)/shard_map/dot_general | solution.py:56
  406.8 35.5 %while.14 = (s32[]{:T(128)}, bf16[8,512,128]{2,1,0:T(8,128)(2,1)S(1)}, s32[8]{0:T(128)S(1)}, bf16[8,512,128]{2,1,0:T(8,128)(2,1)S(1)}, bf16[2560,128]{1,0:T(8,12...) while((s32[]{:T(128)}, ...), condition=%wide.region_6.7_spmd.clone, body=%wide.region_3.6_spmd.clone.sunk | while | flops 681973248 | bytes 17850196 | solution.py:127
  412.8 1.1 fusion.58
  417.3 1.1 fusion.58
  421.7 1.1 fusion.58
  443.1 1.2 copy.55
  (116 shorter events, 46.4 us)
Async XLA Ops:
  7.2 8.6 %copy-start = (s32[64,16]{0,1:T(8,128)S(1)}, s32[64,16]{0,1:T(8,128)}, u32[]{:S(2)}) copy-start(s32[64,16]{0,1:T(8,128)} %param.21) | copy-start | bytes 12292
  7.2 16.3 %copy-start.4 = (bf16[1024,128]{1,0:T(8,128)(2,1)S(1)}, bf16[1024,128]{1,0:T(8,128)(2,1)}, u32[]{:S(2)}) copy-start(bf16[1024,128]{1,0:T(8,128)(2,1)} %param.19) | copy-start | bytes 786436
  7.2 106.5 %all-gather.9.cloned.1.call-start = ((), (), s32[]{:S(2)}) async-start(), calls=%async_computation.2 | async-start | bytes 1056768 | tf_op jit(solution)/shard_map/all_gather | solution.py:59
  7.9 127.2 %all-gather.5.cloned.1.call-start = ((), (), s32[]{:S(2)}) async-start(), calls=%async_computation | async-start | bytes 3145728 | tf_op jit(solution)/shard_map/all_gather | solution.py:52
  8.7 229.0 %all-gather.11.cloned.1.call-start = ((), (), s32[]{:S(2)}) async-start(), calls=%async_computation.3 | async-start | bytes 1056768 | tf_op jit(solution)/shard_map/all_gather | solution.py:60
  9.4 384.9 %all-gather.7.cloned.1.call-start = ((), (), s32[]{:S(2)}) async-start(), calls=%async_computation.1 | async-start | bytes 16908288 | tf_op jit(solution)/shard_map/all_gather | solution.py:58
  10.0 7.8 %collective-permute-start = (bf16[1024,128]{1,0:T(8,128)(2,1)}, bf16[1024,128]{1,0:T(8,128)(2,1)S(1)}, u32[]{:S(2)}, u32[]{:S(2)}) collective-permute-start(bf16[1024,128]{1,0:T(8,128)(2,1)} %param.18), channel_id=1, source_target_pairs={{0,2},{2,0},{4,6},{6,4},{8,10},{10,8},{12,14},{14,12},{16,18},{18,... | collective-permute-start | bytes 786440 | tf_op jit(solution)/shard_map/ppermute | solution.py:14
  12.5 10.9 %collective-permute-start.2 = (bf16[1024,128]{1,0:T(8,128)(2,1)}, bf16[1024,128]{1,0:T(8,128)(2,1)S(1)}, u32[]{:S(2)}, u32[]{:S(2)}) collective-permute-start(bf16[1024,128]{1,0:T(8,128)(2,1)} %param.19), channel_id=1, source_target_pairs={{0,2},{2,0},{4,6},{6,4},{8,10},{10,8},{12,14},{14,12},{16,18},{18,... | collective-permute-start | bytes 786440 | tf_op jit(solution)/shard_map/ppermute | solution.py:14
  14.5 4.5 copy-start.5
  135.2 3.6 copy-start.6
  135.2 102.5 %copy-start.1 = (bf16[256,4096]{1,0:T(8,128)(2,1)S(1)}, bf16[256,4096]{1,0:T(8,128)(2,1)}, u32[]{:S(2)}) copy-start(bf16[256,4096]{1,0:T(8,128)(2,1)} %all-gather.5.cloned.1.call-done) | copy-start | bytes 6291460
  139.7 103.5 %collective-permute-start.1 = (bf16[256,128]{0,1:T(8,128)(2,1)}, bf16[256,128]{0,1:T(8,128)(2,1)}, u32[]{:S(2)}, u32[]{:S(2)}) collective-permute-start(bf16[256,128]{0,1:T(8,128)(2,1)} %pad_maximum_fusion.2), channel_id=1, source_target_pairs={{0,2},{2,0},{4,6},{6,4},{8,10},{10,8},{12,14},{14,12},{16,18},{18,... | collective-permute-start | bytes 196616 | tf_op jit(solution)/shard_map/ppermute | solution.py:14
  242.0 4.4 collective-permute-start.3
  402.9 0.8 copy-start.7
  405.4 1.2 copy-start.2
  405.4 1.4 copy-start.3
  405.4 1.4 copy-start.8
Sparse Core Ops, SparseCore 0:
  11.4 102.2 all-gather.8
  115.5 19.6 all-gather.4
  138.6 99.0 all-gather.10
  241.1 153.1 all-gather.6
where the time goes:
time: 451 us
  waiting for transfers between devices  358 us (79%)
  matrix products  29.2 us (6%)
  other arithmetic  27.5 us (6%)
  local copies, waits for them, and re-layouts  15.7 us (3%)
  between operations  14.7 us (3%)
  starting transfers between devices  4.99 us (1%)
    all_gather x1, waiting for transfers between devices, on_device(): query = add_rows(lax.all_gather(w_query, 'ctx', axis=0, tiled=True))  142 us
    all_gather x1, waiting for transfers between devices, on_device(): lax.all_gather(value_weight, 'ctx', axis=0, tiled=True)  96.9 us
    all_gather x1, waiting for transfers between devices, on_device(): lax.all_gather(key_weight, 'ctx', axis=0, tiled=True)  90.1 us
    all_gather x1, waiting for transfers between devices, on_device(): whole = lax.all_gather(hidden, 'tp', axis=1, tiled=True)  21.4 us
    dot_general x3, matrix products, add_rows(): return jnp.dot(whole, piece, preferred_element_type=jnp.float32)  13.1 us
  transfers between devices with their start and end apart: 8, of which 6 were waited for; matrix products, arithmetic and copies ran while one was open for 5% of the time, Pallas kernels for 0%

commit v1 on v0

--- a/solution.py
+++ b/solution.py
@@ -57,7 +57,11 @@
 
     query = add_rows(lax.all_gather(w_query, "ctx", axis=0, tiled=True))
     key_projected = add_rows(lax.all_gather(key_weight, "ctx", axis=0, tiled=True))
-    value_projected = add_rows(lax.all_gather(value_weight, "ctx", axis=0, tiled=True))
+    value_projected = add_rows(
+        jnp.concatenate(
+            lax.all_to_all(jnp.stack([value_weight] * lax.axis_size("ctx")), "ctx", 0, 0), axis=0
+        )
+    )
     heads_q = w_query.shape[1] // HEAD_SIZE
     heads_kv = key_weight.shape[1] // HEAD_SIZE
     count = lax.dynamic_index_in_dim(counts, traj_id, 0, keepdims=False)

time: 451 us -> 349 us (0.77)
  waiting for transfers between devices: 358 us -> 241 us
  starting transfers between devices: 4.99 us -> 20 us
    all_gather x1 -> x0, waiting for transfers between devices: 96.9 us -> none  [on_device(): lax.all_gather(value_weight, 'ctx', axis=0, tiled=True)]
    all_to_all x0 -> x1, starting transfers between devices: none -> 15.8 us  [on_device(): lax.all_to_all(jnp.stack([value_weight] * lax.axis_size('ctx')), 'ctx', 0...]
    all_gather x1, waiting for transfers between devices: 90.1 us -> 82.6 us  [on_device(): lax.all_gather(key_weight, 'ctx', axis=0, tiled=True)]
    all_gather x1, waiting for transfers between devices: 142 us -> 135 us  [on_device(): query = add_rows(lax.all_gather(w_query, 'ctx', axis=0, tiled=True))]
    ppermute x4, waiting for transfers between devices: 5.59 us -> 0.01 us  [from_partner(): return lax.ppermute(value, axis, pairs)]
  transfers between devices with their start and end apart: 8 -> 8, of which waited for: 6 -> 3; matrix products, arithmetic and copies ran while one was open for 5% -> 7% of each run, Pallas kernels for 0% -> 0%
where the time goes in v1:
time: 349 us; the launch traced here: 348 us
  waiting for transfers between devices  241 us (69%)
  matrix products  29.2 us (8%)
  other arithmetic  26.5 us (8%)
  starting transfers between devices  20 us (6%)
  local copies, waits for them, and re-layouts  16.9 us (5%)
  between operations  14.7 us (4%)
    all_gather x1, waiting for transfers between devices, on_device(): query = add_rows(lax.all_gather(w_query, 'ctx', axis=0, tiled=True))  135 us
    all_gather x1, waiting for transfers between devices, on_device(): lax.all_gather(key_weight, 'ctx', axis=0, tiled=True)  82.6 us
    all_gather x1, waiting for transfers between devices, on_device(): whole = lax.all_gather(hidden, 'tp', axis=1, tiled=True)  21.4 us
    all_to_all x1, starting transfers between devices, on_device(): lax.all_to_all(jnp.stack([value_weight] * lax.axis_size('ctx')), 'ctx', 0...  15.8 us
    dot_general x3, matrix products, add_rows(): return jnp.dot(whole, piece, preferred_element_type=jnp.float32)  13.1 us
    dot_general x8, matrix products, attend(): lax.dot_general(block, keys_all, (((1,), (1,)), ((), ())), preferred_elem...  8.42 us
    dot_general x8, matrix products, attend(): jnp.dot(weight.astype(jnp.bfloat16), vals_all, preferred_element_type=jnp...  7.71 us
  transfers between devices with their start and end apart: 8, of which 3 were waited for; matrix products, arithmetic and copies ran while one was open for 7% of the time, Pallas kernels for 0%

profile of v1, /device:TPU:1, one launch (start us, length us, event | category | flops | bytes accessed | tf_op | source)
XLA Modules:
  0.0 348.3 jit_solution(1175248514359856489)
XLA Ops:
  9.4 2.6 collective-permute-start
  12.1 1.8 stack.2
  13.9 15.8 %all-to-all-start = ((bf16[128,32,128]{2,1,0:T(8,128)(2,1)}), bf16[128,32,128]{2,1,0:T(8,128)(2,1)}, u32[]{:S(2)}, u32[]{:S(2)}) async-start(bf16[128,32,128]{2,1,0:T(8,128)(2,1)} %stack.2), calls=%async_computation | async-start | bytes 2097152 | tf_op jit(solution)/shard_map/all_to_all | solution.py:62
  33.4 82.6 %all-gather.8.cloned.1.call-done = bf16[4096,128]{1,0:T(8,128)(2,1)} async-done(((bf16[32,128]{1,0:T(8,128)(2,1)}), bf16[4096,128]{1,0:T(8,128)(2,1)}) %all-gather.8.cloned.1.call-update) | async-done | bytes 1048592 | tf_op jit(solution)/shard_map/all_gather | solution.py:59
  116.0 21.4 %all-gather.4.cloned.1.call-done = bf16[256,4096]{1,0:T(8,128)(2,1)} async-done(((bf16[256,2048]{1,0:T(8,128)(2,1)}), bf16[256,4096]{1,0:T(8,128)(2,1)}) %all-gather.4.cloned.1.call-update) | async-done | bytes 2097168 | tf_op jit(solution)/shard_map/all_gather | solution.py:52
  137.4 2.8 multiply_reduce_fusion.1
  143.0 2.1 convolution_convert_fusion
  145.1 1.6 copy.49
  147.9 1.6 maximum_select_fusion.2
  149.5 1.7 copy.45
  151.1 1.6 maximum_select_fusion.3
  152.7 1.7 copy.47
  154.4 1.8 pad_maximum_fusion
  157.1 134.6 %all-gather.6.cloned.1.call-done = bf16[4096,2048]{1,0:T(8,128)(2,1)} async-done(((bf16[32,2048]{1,0:T(8,128)(2,1)}), bf16[4096,2048]{1,0:T(8,128)(2,1)}) %all-gather.6.cloned.1.call-update) | async-done | bytes 16777232 | tf_op jit(solution)/shard_map/all_gather | solution.py:58
  291.8 8.2 %convolution_bitcast_fusion = f32[32,8,16,128]{3,1,2,0:T(8,128)S(1)} fusion(bf16[256,4096]{1,0:T(8,128)(2,1)S(1)} %copy-done.1, bf16[4096,2048]{1,0:T(8,128)(2,1)} %all-gather.6.cloned.1.call-done), kind=kOutput, calls=%fused_computation.26 | convolution fusion | flops 4294967296 | bytes 20971520 | tf_op jit(solution)/shard_map/dot_general | solution.py:56
  304.3 35.5 %while.14 = (s32[]{:T(128)}, bf16[8,512,128]{2,1,0:T(8,128)(2,1)S(1)}, s32[8]{0:T(128)S(1)}, bf16[8,512,128]{2,1,0:T(8,128)(2,1)S(1)}, bf16[2560,128]{1,0:T(8,12...) while((s32[]{:T(128)}, ...), condition=%wide.region_6.7_spmd.clone, body=%wide.region_3.6_spmd.clone.sunk | while | flops 681973248 | bytes 17850196 | solution.py:131
  305.9 1.1 fusion.58
  310.3 1.1 fusion.58
  314.8 1.1 fusion.58
  319.2 1.1 fusion.58
  323.6 1.1 fusion.58
  328.1 1.1 fusion.58
  337.0 1.1 fusion.58
  340.5 1.2 copy.55
  (120 shorter events, 42.9 us)
Async XLA Ops:
  7.2 25.0 %copy-start = (s32[64,16]{0,1:T(8,128)S(1)}, s32[64,16]{0,1:T(8,128)}, u32[]{:S(2)}) copy-start(s32[64,16]{0,1:T(8,128)} %param.21) | copy-start | bytes 12292
  7.2 108.8 %all-gather.8.cloned.1.call-start = ((), (), s32[]{:S(2)}) async-start(), calls=%async_computation.3 | async-start | bytes 1056768 | tf_op jit(solution)/shard_map/all_gather | solution.py:59
  7.9 21.8 %copy-start.9 = (s32[64]{0:T(128)S(1)}, s32[64]{0:T(128)}, u32[]{:S(2)}) copy-start(s32[64]{0:T(128)} %param.20) | copy-start | bytes 772
  7.9 25.1 %copy-start.4 = (bf16[1024,128]{1,0:T(8,128)(2,1)S(1)}, bf16[1024,128]{1,0:T(8,128)(2,1)}, u32[]{:S(2)}) copy-start(bf16[1024,128]{1,0:T(8,128)(2,1)} %param.18) | copy-start | bytes 786436
  7.9 129.5 %all-gather.4.cloned.1.call-start = ((), (), s32[]{:S(2)}) async-start(), calls=%async_computation.1 | async-start | bytes 3145728 | tf_op jit(solution)/shard_map/all_gather | solution.py:52
  8.7 283.1 %all-gather.6.cloned.1.call-start = ((), (), s32[]{:S(2)}) async-start(), calls=%async_computation.2 | async-start | bytes 16908288 | tf_op jit(solution)/shard_map/all_gather | solution.py:58
  9.4 23.8 %copy-start.5 = (bf16[1024,128]{1,0:T(8,128)(2,1)S(1)}, bf16[1024,128]{1,0:T(8,128)(2,1)}, u32[]{:S(2)}) copy-start(bf16[1024,128]{1,0:T(8,128)(2,1)} %param.19) | copy-start | bytes 786436
  9.4 23.6 %collective-permute-start = (bf16[1024,128]{1,0:T(8,128)(2,1)}, bf16[1024,128]{1,0:T(8,128)(2,1)S(1)}, u32[]{:S(2)}, u32[]{:S(2)}) collective-permute-start(bf16[1024,128]{1,0:T(8,128)(2,1)} %param.18), channel_id=1, source_target_pairs={{0,2},{2,0},{4,6},{6,4},{8,10},{10,8},{12,14},{14,12},{16,18},{18,... | collective-permute-start | bytes 786440 | tf_op jit(solution)/shard_map/ppermute | solution.py:14
  12.0 21.2 %collective-permute-start.2 = (bf16[1024,128]{1,0:T(8,128)(2,1)}, bf16[1024,128]{1,0:T(8,128)(2,1)S(1)}, u32[]{:S(2)}, u32[]{:S(2)}) collective-permute-start(bf16[1024,128]{1,0:T(8,128)(2,1)} %param.19), channel_id=1, source_target_pairs={{0,2},{2,0},{4,6},{6,4},{8,10},{10,8},{12,14},{14,12},{16,18},{18,... | collective-permute-start | bytes 786440 | tf_op jit(solution)/shard_map/ppermute | solution.py:14
  13.9 129.1 %all-to-all-start = ((bf16[128,32,128]{2,1,0:T(8,128)(2,1)}), bf16[128,32,128]{2,1,0:T(8,128)(2,1)}, u32[]{:S(2)}, u32[]{:S(2)}) async-start(bf16[128,32,128]{2,1,0:T(8,128)(2,1)} %stack.2), calls=%async_computation | async-start | bytes 2097152 | tf_op jit(solution)/shard_map/all_to_all | solution.py:62
  31.0 85.0 %copy-start.6 = (f32[64]{0:T(128)}, f32[64]{0:T(128)S(1)}, u32[]{:S(2)}) copy-start(f32[64]{0:T(128)S(1)} %multiply_exponential_fusion) | copy-start | bytes 772
  137.4 3.6 %copy-start.7 = (f32[64]{0:T(128)S(1)}, f32[64]{0:T(128)}, u32[]{:S(2)}) copy-start(f32[64]{0:T(128)} %copy-done.6) | copy-start | bytes 772
  137.4 5.6 %copy-start.1 = (bf16[256,4096]{1,0:T(8,128)(2,1)S(1)}, bf16[256,4096]{1,0:T(8,128)(2,1)}, u32[]{:S(2)}) copy-start(bf16[256,4096]{1,0:T(8,128)(2,1)} %all-gather.4.cloned.1.call-done) | copy-start | bytes 6291460
  142.0 5.9 %collective-permute-start.1 = (bf16[256,128]{0,1:T(8,128)(2,1)}, bf16[256,128]{0,1:T(8,128)(2,1)}, u32[]{:S(2)}, u32[]{:S(2)}) collective-permute-start(bf16[256,128]{0,1:T(8,128)(2,1)} %pad_maximum_fusion.2), channel_id=1, source_target_pairs={{0,2},{2,0},{4,6},{6,4},{8,10},{10,8},{12,14},{14,12},{16,18},{18,... | collective-permute-start | bytes 196616 | tf_op jit(solution)/shard_map/ppermute | solution.py:14
  147.4 3.7 %collective-permute-start.3 = (bf16[256,128]{0,1:T(8,128)(2,1)S(1)}, bf16[256,128]{0,1:T(8,128)(2,1)}, u32[]{:S(2)}, u32[]{:S(2)}) collective-permute-start(bf16[256,128]{0,1:T(8,128)(2,1)S(1)} %convolution_convert_fusion), channel_id=1, source_target_pairs={{0,2},{2,0},{4,6},{6,4},{8,10},{10,8},{12,14},{14,12},{16,18},{18,... | collective-permute-start | bytes 196616 | tf_op jit(solution)/shard_map/ppermute | solution.py:14
  300.4 0.8 copy-start.8
  302.9 1.2 copy-start.2
  302.9 1.4 copy-start.3
  302.9 1.4 copy-start.10
Sparse Core Ops, SparseCore 0:
  11.4 104.4 all-gather.7
  117.8 19.6 all-gather.3
  141.1 150.6 all-gather.5
